TPU v7x, 512 devices: a whole 4x8x8 slice. The times are simulated.
512 devices in a mesh: ty: 32 (over x, z), tx: 16 (over y, core).
Axes of the slice: x: 4, y: 8, z: 8, core: 2. Of those that a mesh axis runs over, the one named last changes fastest.
Arguments:
- stored_eastward_flow: float32 [30, 256, 2048], P(None, 'ty', 'tx'), may hold values from -6 to 6
- stored_northward_flow: float32 [30, 256, 2048], P(None, 'ty', 'tx'), may hold values from -6 to 6
- stored_heat_content: float32 [30, 256, 2048], P(None, 'ty', 'tx'), may hold values from -6 to 6
- ocean_layer_tally: int32 [256, 2048], P('ty', 'tx'), may hold values from 0 to 30, as said below
- eastward_flow_sensitivity: float32 [30, 256, 2048], P(None, 'ty', 'tx'), may hold values from -6 to 6
- northward_flow_sensitivity: float32 [30, 256, 2048], P(None, 'ty', 'tx'), may hold values from -6 to 6
- scalar_content_sensitivity: float32 [30, 256, 2048], P(None, 'ty', 'tx'), may hold values from -6 to 6
- elevation_sensitivity: float32 [256, 2048], P('ty', 'tx'), may hold values from -6 to 6
Outputs:
- u_gradient: float32 [30, 256, 2048], P(None, 'ty', 'tx')
- v_gradient: float32 [30, 256, 2048], P(None, 'ty', 'tx')
- t_gradient: float32 [30, 256, 2048], P(None, 'ty', 'tx')
- eta_gradient: float32 [256, 2048], P('ty', 'tx')
Inputs may be any that keep to these rules, and one draw needn't show every extreme that they name: `ocean_layer_tally`: the number of wet levels of each column; 0 marks land.
All inputs are finite; a program needn't handle non-finite values.
Results may differ from a plain program's by a relative error of at most 0.0001.
Values sent between devices are 32-bit elements; how exact they have to be, the bound alone decides.
A program may use at most 64 MiB of HBM per device.

v0:
```python
import jax
import jax.numpy as jnp
from jax import lax
from jax.sharding import PartitionSpec as P

ITERS = 4


ADVECT = 0.1
GRAVITY_DT = 0.1
STEP_DT = 1.0


def padded(array, sides, width):
    for axis, dim in sides:
        size, length = (lax.axis_size(axis), array.shape[dim])
        up = [(i, (i + 1) % size) for i in range(size - 1)]
        down = [(j, i) for i, j in up]
        last = lax.slice_in_dim(array, length - width, length, axis=dim)
        first = lax.slice_in_dim(array, 0, width, axis=dim)
        before = lax.ppermute(last, axis, up)
        after = lax.ppermute(first, axis, down)
        array = jnp.concatenate([before, array, after], axis=dim)
    return array


def wet_cells(count_float, levels):
    level_index = jnp.arange(levels).astype(jnp.float32)
    return (level_index[:, None, None] < count_float[None]).astype(jnp.float32)


def tendencies(u_input, v_input, t_input, wet_cell, coriolis_u, coriolis_v):
    row_count = u_input.shape[1] - 4
    col_count = u_input.shape[2] - 4

    def offset_view(source, shift_row, shift_col):
        return source[
            :, 2 + shift_row : 2 + shift_row + row_count, 2 + shift_col : 2 + shift_col + col_count
        ]

    def mask_u(shift_row, shift_col):
        return offset_view(wet_cell, shift_row, shift_col) * offset_view(
            wet_cell, shift_row, shift_col - 1
        )

    def mask_v(shift_row, shift_col):
        return offset_view(wet_cell, shift_row, shift_col) * offset_view(
            wet_cell, shift_row - 1, shift_col
        )

    def flux_x(shift_col):
        face_value = (
            7.0 * (offset_view(t_input, 0, shift_col) + offset_view(t_input, 0, shift_col - 1))
            - (offset_view(t_input, 0, shift_col + 1) + offset_view(t_input, 0, shift_col - 2))
        ) / 12.0
        return mask_u(0, shift_col) * offset_view(u_input, 0, shift_col) * face_value

    def flux_y(shift_row):
        face_value = (
            7.0 * (offset_view(t_input, shift_row, 0) + offset_view(t_input, shift_row - 1, 0))
            - (offset_view(t_input, shift_row + 1, 0) + offset_view(t_input, shift_row - 2, 0))
        ) / 12.0
        return mask_v(shift_row, 0) * offset_view(v_input, shift_row, 0) * face_value

    t_new = offset_view(t_input, 0, 0) - ADVECT * offset_view(wet_cell, 0, 0) * (
        flux_x(1) - flux_x(0) + flux_y(1) - flux_y(0)
    )
    u_here = offset_view(u_input, 0, 0)
    v_here = offset_view(v_input, 0, 0)
    v_bar = 0.25 * (
        v_here
        + offset_view(v_input, 1, 0)
        + offset_view(v_input, 0, -1)
        + offset_view(v_input, 1, -1)
    )
    u_bar = 0.25 * (
        u_here
        + offset_view(u_input, 0, 1)
        + offset_view(u_input, -1, 0)
        + offset_view(u_input, -1, 1)
    )
    u_star = u_here + ADVECT * mask_u(0, 0) * (
        coriolis_u * v_bar
        - u_here * 0.5 * (offset_view(u_input, 0, 1) - offset_view(u_input, 0, -1))
        - v_bar * 0.5 * (offset_view(u_input, 1, 0) - offset_view(u_input, -1, 0))
    )
    v_star = v_here + ADVECT * mask_v(0, 0) * (
        -coriolis_v * u_bar
        - u_bar * 0.5 * (offset_view(v_input, 0, 1) - offset_view(v_input, 0, -1))
        - v_here * 0.5 * (offset_view(v_input, 1, 0) - offset_view(v_input, -1, 0))
    )
    return (u_star, v_star, t_new)


def surface_apply(rimmed, depth_u, depth_v):
    centre = rimmed[1:-1, 1:-1]
    east = rimmed[1:-1, 2:]
    west = rimmed[1:-1, :-2]
    north = rimmed[2:, 1:-1]
    south = rimmed[:-2, 1:-1]
    return centre - GRAVITY_DT * STEP_DT * (
        depth_u[1:-1, 2:] * (east - centre)
        - depth_u[1:-1, 1:-1] * (centre - west)
        + depth_v[2:, 1:-1] * (north - centre)
        - depth_v[1:-1, 1:-1] * (centre - south)
    )


def surface_rim(stacked_fields):
    return padded(stacked_fields, (("ty", 1), ("tx", 2)), 1)


def operate(direction, depth_u, depth_v):
    return surface_apply(surface_rim(direction[None])[0], depth_u, depth_v)


def squares(residual):
    return lax.psum(jnp.sum(residual * residual), ("ty", "tx"))


def solve_surface(surface_load, depth_u, depth_v):
    solution = jnp.zeros_like(surface_load)
    residual = surface_load
    direction = surface_load
    norm_now = squares(residual)
    for iteration in range(ITERS):
        applied = operate(direction, depth_u, depth_v)
        curvature = lax.psum(jnp.sum(direction * applied), ("ty", "tx"))
        step_length = norm_now / curvature
        solution = solution + step_length * direction
        residual = residual - step_length * applied
        norm_next = squares(residual)
        direction = residual + norm_next / norm_now * direction
        norm_now = norm_next
    return solution


def on_device(
    stored_eastward_flow,
    stored_northward_flow,
    stored_heat_content,
    ocean_layer_tally,
    eastward_flow_sensitivity,
    northward_flow_sensitivity,
    scalar_content_sensitivity,
    elevation_sensitivity,
):
    levels, row_count, col_count = stored_eastward_flow.shape
    total_rows = row_count * lax.axis_size("ty")
    first_row = (lax.axis_index("ty") * row_count).astype(jnp.float32)
    thickness = (1.0 + jnp.arange(levels).astype(jnp.float32) / levels)[:, None, None]
    layer_number_map = ocean_layer_tally.astype(jnp.float32)[None]
    stacked_fields = jnp.concatenate(
        [stored_eastward_flow, stored_northward_flow, stored_heat_content, layer_number_map], axis=0
    )
    widened = padded(stacked_fields, (("ty", 1), ("tx", 2)), 4)
    u_wide = widened[0:levels]
    v_wide = widened[levels : 2 * levels]
    t_wide = widened[2 * levels : 3 * levels]
    wet_wide = wet_cells(widened[-1], levels)
    inner_wet = wet_wide[:, 3:-3, 3:-3]
    u_mask = inner_wet * wet_wide[:, 3:-3, 2:-4]
    v_mask = inner_wet * wet_wide[:, 2:-4, 3:-3]
    depth_u = jnp.sum(thickness * u_mask, axis=0)
    depth_v = jnp.sum(thickness * v_mask, axis=0)
    col_own = jnp.stack(
        [
            jnp.sum(u_mask[:, 1:-1, 1:-1] * eastward_flow_sensitivity, axis=0),
            jnp.sum(v_mask[:, 1:-1, 1:-1] * northward_flow_sensitivity, axis=0),
        ]
    )
    col_rimmed = surface_rim(col_own)
    col_u = col_rimmed[0]
    col_v = col_rimmed[1]
    surface_load = elevation_sensitivity + GRAVITY_DT * (
        col_u[1:-1, 2:] - col_u[1:-1, 1:-1] + col_v[2:, 1:-1] - col_v[1:-1, 1:-1]
    )
    solution = solve_surface(surface_load, depth_u, depth_v)
    solution_rimmed = surface_rim(solution[None])[0]
    u_own = (
        eastward_flow_sensitivity
        + STEP_DT
        * thickness
        * u_mask[:, 1:-1, 1:-1]
        * (solution - solution_rimmed[1:-1, :-2])[None]
    )
    v_own = (
        northward_flow_sensitivity
        + STEP_DT
        * thickness
        * v_mask[:, 1:-1, 1:-1]
        * (solution - solution_rimmed[:-2, 1:-1])[None]
    )
    cotangent_wide = padded(
        jnp.concatenate([u_own, v_own, scalar_content_sensitivity], axis=0),
        (("ty", 1), ("tx", 2)),
        2,
    )
    u_cotangent = cotangent_wide[0:levels]
    v_cotangent = cotangent_wide[levels : 2 * levels]
    t_cotangent = cotangent_wide[2 * levels : 3 * levels]
    row_global = first_row - 2.0 + jnp.arange(row_count + 4).astype(jnp.float32)
    coriolis_u = (0.5 + (row_global + 0.5) / total_rows)[:, None]
    coriolis_v = (0.5 + row_global / total_rows)[:, None]

    def advance_ocean_once(u_input, v_input, t_input):
        return tendencies(u_input, v_input, t_input, wet_wide, coriolis_u, coriolis_v)

    advance_results, backward_chain_rule = jax.vjp(advance_ocean_once, u_wide, v_wide, t_wide)
    gradients = backward_chain_rule((u_cotangent, v_cotangent, t_cotangent))
    return (
        gradients[0][:, 4:-4, 4:-4],
        gradients[1][:, 4:-4, 4:-4],
        gradients[2][:, 4:-4, 4:-4],
        solution,
    )


def solution(mesh):
    placed = (
        P(None, "ty", "tx"),
        P(None, "ty", "tx"),
        P(None, "ty", "tx"),
        P("ty", "tx"),
        P(None, "ty", "tx"),
        P(None, "ty", "tx"),
        P(None, "ty", "tx"),
        P("ty", "tx"),
    )
    return jax.shard_map(
        on_device,
        mesh=mesh,
        in_specs=placed,
        out_specs=(P(None, "ty", "tx"), P(None, "ty", "tx"), P(None, "ty", "tx"), P("ty", "tx")),
        check_vma=False,
    )
```

profile of v0, /device:TPU:1, one launch (start us, length us, event | category | flops | bytes accessed | tf_op | source)
XLA Modules:
  0.0 879.1 jit_solution(7684287407095664608)
XLA Ops:
  2.5 4.8 collective-permute-start
  9.8 4.5 collective-permute-done.1
  15.7 5.8 collective-permute-start.3
  21.5 1.9 collective-permute-start.2
  25.5 2.1 pad_maximum_fusion
  29.2 3.8 collective-permute-start.4
  34.4 4.9 collective-permute-done.5
  39.3 5.4 collective-permute-start.6
  44.7 1.9 collective-permute-start.7
  46.6 3.1 collective-permute-done.7
  49.9 4.6 collective-permute-start.8
  55.8 3.3 collective-permute-done.9
  59.1 3.1 collective-permute-start.10
  62.2 1.9 collective-permute-start.11
  64.2 3.0 collective-permute-done.11
  68.0 104.1 %all-reduce.37 = (f32[]{:T(128)}, f32[]{:T(128)}) all-reduce(f32[]{:T(128)} %get-tuple-element.9, f32[]{:T(128)} %get-tuple-element.8), channel_id=1, replica_groups=mesh['ty'=32,'tx'=16] {'ty','tx'}, use_global_device_ids=true, to_apply=%region_3.0 | all-reduce | flops 2 | bytes 16 | tf_op jit(solution)/shard_map/psum | solution.py:118
  174.0 95.7 %psum.58 = f32[]{:T(128)} all-reduce(f32[]{:T(128)} %multiply_reduce_fusion.8), channel_id=1, replica_groups=mesh['ty'=32,'tx'=16] {'ty','tx'}, use_global_device_ids=true, to_apply=%region_9.0 | all-reduce | flops 1 | bytes 8 | tf_op jit(solution)/shard_map/psum | solution.py:118
  271.0 1.6 collective-permute-start.12
  274.0 3.0 collective-permute-done.13
  277.0 4.8 collective-permute-start.14
  281.8 1.9 collective-permute-start.15
  283.8 3.0 collective-permute-done.15
  287.6 100.4 %psum.59 = f32[]{:T(128)} all-reduce(f32[]{:T(128)} %get-tuple-element.41), channel_id=1, replica_groups=mesh['ty'=32,'tx'=16] {'ty','tx'}, use_global_device_ids=true, to_apply=%region_11.0 | all-reduce | flops 1 | bytes 8 | tf_op jit(solution)/shard_map/psum | solution.py:128
  389.9 95.7 %psum.60 = f32[]{:T(128)} all-reduce(f32[]{:T(128)} %get-tuple-element.39), channel_id=1, replica_groups=mesh['ty'=32,'tx'=16] {'ty','tx'}, use_global_device_ids=true, to_apply=%region_13.0 | all-reduce | flops 1 | bytes 8 | tf_op jit(solution)/shard_map/psum | solution.py:118
  487.0 1.6 collective-permute-start.16
  489.9 3.0 collective-permute-done.17
  493.0 4.8 collective-permute-start.18
  497.8 1.9 collective-permute-start.19
  499.7 3.0 collective-permute-done.19
  503.5 100.4 %psum.61 = f32[]{:T(128)} all-reduce(f32[]{:T(128)} %get-tuple-element.37), channel_id=1, replica_groups=mesh['ty'=32,'tx'=16] {'ty','tx'}, use_global_device_ids=true, to_apply=%region_15.0 | all-reduce | flops 1 | bytes 8 | tf_op jit(solution)/shard_map/psum | solution.py:128
  605.9 95.7 %psum.62 = f32[]{:T(128)} all-reduce(f32[]{:T(128)} %multiply_reduce_fusion.4), channel_id=1, replica_groups=mesh['ty'=32,'tx'=16] {'ty','tx'}, use_global_device_ids=true, to_apply=%region_17.0 | all-reduce | flops 1 | bytes 8 | tf_op jit(solution)/shard_map/psum | solution.py:118
  702.9 1.6 collective-permute-start.20
  705.9 3.0 collective-permute-done.21
  708.9 4.8 collective-permute-start.22
  713.7 1.9 collective-permute-start.23
  715.7 3.0 collective-permute-done.23
  719.5 100.4 %psum.63 = f32[]{:T(128)} all-reduce(f32[]{:T(128)} %fusion.43), channel_id=1, replica_groups=mesh['ty'=32,'tx'=16] {'ty','tx'}, use_global_device_ids=true, to_apply=%region_19.0 | all-reduce | flops 1 | bytes 8 | tf_op jit(solution)/shard_map/psum | solution.py:128
  823.9 3.0 collective-permute-done.25
  826.9 6.2 collective-permute-start.26
  833.1 1.9 collective-permute-start.27
  835.1 3.0 collective-permute-done.27
  840.4 1.7 pad_maximum_fusion.19
  842.1 2.3 collective-permute-start.28
  845.7 4.3 collective-permute-done.29
  855.4 1.9 collective-permute-start.31
  857.4 3.8 collective-permute-start.30
  864.4 2.5 pad_maximum_fusion.1
  867.4 1.5 multiply_negate_fusion.2
  (138 shorter events, 46.7 us)
Async XLA Ops:
  0.6 13.7 %copy-start = (f32[30,8,128]{2,1,0:T(8,128)S(1)}, f32[30,8,128]{2,1,0:T(8,128)}, u32[]{:S(2)}) copy-start(f32[30,8,128]{2,1,0:T(8,128)} %param.10) | copy-start | bytes 368644
  0.6 13.7 %copy-start.2 = (f32[30,8,128]{2,1,0:T(8,128)S(1)}, f32[30,8,128]{2,1,0:T(8,128)}, u32[]{:S(2)}) copy-start(f32[30,8,128]{2,1,0:T(8,128)} %param.9) | copy-start | bytes 368644
  0.7 13.7 %copy-start.4 = (f32[30,8,128]{2,1,0:T(8,128)S(1)}, f32[30,8,128]{2,1,0:T(8,128)}, u32[]{:S(2)}) copy-start(f32[30,8,128]{2,1,0:T(8,128)} %param.8) | copy-start | bytes 368644
  2.5 7.3 collective-permute-start
  7.4 6.9 collective-permute-start.1
  9.8 15.2 %copy-start.6 = (f32[91,4,128]{2,1,0:T(4,128)}, f32[91,4,128]{2,1,0:T(4,128)S(1)}, u32[]{:S(2)}) copy-start(f32[91,4,128]{2,1,0:T(4,128)S(1)} %collective-permute-done) | copy-start | bytes 559108
  15.7 9.3 %collective-permute-start.3 = (f32[91,16,4]{0,1,2:T(8,128)S(1)}, f32[91,16,4]{0,1,2:T(8,128)S(1)}, u32[]{:S(2)}, u32[]{:S(2)}) collective-permute-start(f32[91,16,4]{0,1,2:T(8,128)S(1)} %copy.27), channel_id=1, source_target_pairs={{1,0},{2,1},{3,2},{4,3},{5,4},{6,5},{7,6},{8,7},{9,8},{10,9},{11,1... | collective-permute-start | bytes 69896 | tf_op jit(solution)/shard_map/ppermute | solution.py:22
  21.5 3.1 collective-permute-start.2
  27.6 1.4 copy-start.14
  27.6 1.4 copy-start.15
  27.7 22.1 %copy-start.17 = (f32[8,128]{1,0:T(8,128)S(1)}, f32[8,128]{1,0:T(8,128)}, u32[]{:S(2)}) copy-start(f32[8,128]{1,0:T(8,128)} %param.15) | copy-start | bytes 12292
  28.2 0.8 copy-start.12
  28.2 1.0 copy-start.13
  29.2 5.1 collective-permute-start.4
  33.0 6.2 collective-permute-start.5
  39.3 7.3 collective-permute-start.6
  44.7 5.1 collective-permute-start.7
  49.9 5.9 collective-permute-start.8
  54.5 4.6 collective-permute-start.9
  59.1 5.0 collective-permute-start.10
  62.2 5.0 collective-permute-start.11
  271.0 2.9 collective-permute-start.12
  272.7 4.3 collective-permute-start.13
  277.0 6.7 collective-permute-start.14
  281.8 5.0 collective-permute-start.15
  487.0 2.9 collective-permute-start.16
  488.6 4.3 collective-permute-start.17
  493.0 6.7 collective-permute-start.18
  497.8 5.0 collective-permute-start.19
  702.9 2.9 collective-permute-start.20
  704.5 4.3 collective-permute-start.21
  708.9 6.7 collective-permute-start.22
  713.7 5.0 collective-permute-start.23
  821.2 31.3 %copy-start.16 = (f32[8,128]{1,0:T(8,128)}, f32[8,128]{1,0:T(8,128)S(1)}, u32[]{:S(2)}) copy-start(f32[8,128]{1,0:T(8,128)S(1)} %multiply_add_fusion.2) | copy-start | bytes 12292
  821.2 2.6 collective-permute-start.24
  822.5 4.3 collective-permute-start.25
  826.9 8.2 collective-permute-start.26
  833.1 5.0 collective-permute-start.27
  839.7 2.3 copy-start.11
  842.1 3.6 collective-permute-start.28
  844.3 5.6 collective-permute-start.29
  855.4 7.7 collective-permute-start.31
  857.4 4.5 collective-permute-start.30
  870.7 1.2 copy-start.1
  870.8 1.2 copy-start.3
  870.8 1.2 copy-start.5
  870.8 1.2 copy-start.7
  870.8 1.2 copy-start.9
  (2 other events, 1.3 us)
where the time goes:
time: 887 us; the launch traced here: 879 us
  blocking collectives  692 us (78%)
  starting transfers between devices  85.9 us (10%)
  waiting for transfers between devices  50 us (6%)
  other arithmetic  28.9 us (3%)
  local copies, waits for them, and re-layouts  10.9 us (1%)
  between operations  10.9 us (1%)
    psum x4, blocking collectives, squares(): return lax.psum(jnp.sum(residual * residual), ('ty', 'tx'))  391 us
    psum x3, blocking collectives, solve_surface(): curvature = lax.psum(jnp.sum(direction * applied), ('ty', 'tx'))  301 us
    ppermute x16, starting transfers between devices, padded(): before = lax.ppermute(last, axis, up)  56.4 us
    ppermute x16, waiting for transfers between devices, padded(): after = lax.ppermute(first, axis, down)  47 us
    ppermute x16, starting transfers between devices, padded(): after = lax.ppermute(first, axis, down)  29.5 us
  transfers between devices with their start and end apart: 32, of which 17 were waited for; matrix products, arithmetic and copies ran while one was open for 0% of the time, Pallas kernels for 0%

commit v1 on v0

v1 whole, which is shorter than its diff:
```python
import functools

import jax
import jax.numpy as jnp
from jax import lax
from jax.experimental import pallas as pl
from jax.experimental.pallas import tpu as pltpu
from jax.sharding import PartitionSpec as P

MESH = pl.DeviceIdType.MESH
ADVECT = 0.1
GRAVITY_DT = 0.1
ROWS, COLS = 8, 128

E, W, N, S, NE, NW, SE, SW = range(8)
WAY = ((0, 1), (0, -1), (1, 0), (-1, 0), (1, 1), (1, -1), (-1, 1), (-1, -1))
OPPOSITE = (W, E, S, N, SW, SE, NW, NE)
COLUMN_SLOT = {E: 0, W: 1, NE: 2, NW: 3, SE: 4, SW: 5}


def turn(x, shift, axis):
    return pltpu.roll(x, shift % x.shape[axis], axis)


def east(x):
    return turn(x, -1, 1)


def west(x):
    return turn(x, 1, 1)


def north(x):
    return turn(x, -1, 0)


def south(x):
    return turn(x, 1, 0)


def tile(a, b, c, d):
    return jnp.concatenate(
        [jnp.concatenate([a, b], axis=1), jnp.concatenate([c, d], axis=1)], axis=0
    )


def kernel(
    levels, n_ty, n_tx,
    u_ref, v_ref, t_ref, count_ref, us_ref, vs_ref, ts_ref, elev_ref,
    gu_ref, gv_ref, gt_ref, eta_ref,
    count_in, elev_in, col_out, col_in,
    colp_out, colp_in, rown_out, rows_out, rown2_out, rows2_out,
    rown_in, rows_in, rown2_in, rows2_in,
    sides, corners, mine, tx_in, ty_in,
    k_pu, k_pv, k_b, k_qv, k_qu, k_c, k_u, k_v,
    hop_send, hop_recv, tx_send, tx_recv, ty_send, ty_recv,
):
    r, c = lax.axis_index("ty"), lax.axis_index("tx")
    total_rows = ROWS * n_ty

    def at(d):
        dy, dx = WAY[d]
        return (lax.rem(r + dy + n_ty, n_ty), lax.rem(c + dx + n_tx, n_tx))

    def hop(number, src, dst, d):
        return pltpu.make_async_remote_copy(
            src_ref=src, dst_ref=dst,
            send_sem=hop_send.at[number], recv_sem=hop_recv.at[number],
            device_id=at(d), device_id_type=MESH,
        )

    barrier = pltpu.get_barrier_semaphore()

    def greet_tx(o, carry):
        pl.semaphore_signal(barrier, inc=1, device_id=(r, lax.rem(c + o, n_tx)), device_id_type=MESH)
        return carry

    def greet_ty(o, carry):
        pl.semaphore_signal(barrier, inc=1, device_id=(lax.rem(r + o, n_ty), c), device_id_type=MESH)
        return carry

    lax.fori_loop(1, n_ty, greet_ty, 0)
    lax.fori_loop(1, n_tx, greet_tx, 0)
    for d in (NE, NW, SE, SW):
        pl.semaphore_signal(barrier, inc=1, device_id=at(d), device_id_type=MESH)

    lane = lax.broadcasted_iota(jnp.int32, (ROWS, COLS), 1)
    sub = lax.broadcasted_iota(jnp.int32, (ROWS, COLS), 0)
    fields = (u_ref, v_ref, us_ref, vs_ref, t_ref, ts_ref)

    def pack(k, packed):
        x = [f[k] for f in fields]
        here = lax.div(lane, 4) == k
        shift = lax.rem(4 * k + 2, COLS)
        packed = tuple(jnp.where(here, pltpu.roll(a, shift, 1), b) for a, b in zip(x, packed))
        u, v, us, vs, t, ts = x
        rown_out[k] = jnp.where(
            sub >= 6, u, jnp.where(sub >= 4, turn(v, -2, 0), jnp.where(sub >= 2, turn(t, 4, 0), turn(ts, 2, 0)))
        )
        rows_out[k] = jnp.where(
            sub < 2, u, jnp.where(sub < 4, turn(v, 2, 0), jnp.where(sub < 6, turn(t, 4, 0), turn(ts, -2, 0)))
        )
        rown2_out[k] = jnp.concatenate([us[7:8], vs[7:8]], axis=0)
        rows2_out[k] = jnp.concatenate([us[0:1], vs[0:1]], axis=0)
        return packed

    packed = lax.fori_loop(0, levels, pack, tuple(jnp.zeros((ROWS, COLS), jnp.float32) for _ in fields))
    for f in range(6):
        colp_out[f] = packed[f]

    pl.semaphore_wait(barrier, (n_tx - 1) + (n_ty - 1) + 4)

    first = [hop(d, count_ref, count_in.at[OPPOSITE[d]], d) for d in range(8)]
    first += [hop(8 + d, elev_ref, elev_in.at[OPPOSITE[d]], d) for d in range(8)]
    for copy in first:
        copy.start()

    wide_row = lax.broadcasted_iota(jnp.int32, (3 * ROWS, 2 * COLS), 0)
    wide_col = lax.broadcasted_iota(jnp.int32, (3 * ROWS, 2 * COLS), 1)
    row_at = r * ROWS + jnp.where(wide_row < 16, wide_row, wide_row - 24)
    col_at = c * COLS + jnp.where(wide_col < 192, wide_col, wide_col - 256)
    inside = (row_at >= 0) & (row_at < total_rows) & (col_at >= 0) & (col_at < COLS * n_tx)

    def around(own, part):
        rim = [jnp.where(lane < 64, part(a), part(b)) for a, b in ((E, W), (NE, NW), (SE, SW))]
        return jnp.concatenate(
            [jnp.concatenate([a, b], axis=1) for a, b in zip((own, part(N), part(S)), rim)], axis=0
        )

    for copy in first:
        copy.wait_recv()
    count = jnp.where(inside, around(count_ref[...], lambda d: count_in[d]).astype(jnp.float32), 0.0)
    count_u = jnp.minimum(count, west(count))
    count_v = jnp.minimum(count, south(count))
    depth_u = count_u + count_u * (count_u - 1.0) * (0.5 / levels)
    depth_v = count_v + count_v * (count_v - 1.0) * (0.5 / levels)

    own_u, own_v = count_u[:ROWS, :COLS], count_v[:ROWS, :COLS]
    col_u = jnp.zeros((ROWS, COLS), jnp.float32)
    col_v = jnp.zeros((ROWS, COLS), jnp.float32)
    for k in range(levels):
        col_u = col_u + jnp.where(own_u > float(k), us_ref[k], 0.0)
        col_v = col_v + jnp.where(own_v > float(k), vs_ref[k], 0.0)
    col_out[0] = col_u
    col_out[1] = col_v
    second = [hop(16 + d, col_out, col_in.at[OPPOSITE[d]], d) for d in range(8)]
    for copy in second:
        copy.start()

    third = [
        hop(24, rown_out, rows_in, N), hop(25, rows_out, rown_in, S),
        hop(26, rown2_out, rows2_in, N), hop(27, rows2_out, rown2_in, S),
    ]
    for i, d in enumerate((E, W, NE, NW, SE, SW)):
        slot = colp_in.at[COLUMN_SLOT[OPPOSITE[d]]]
        whole = d in (E, W)
        third.append(
            hop(28 + i, colp_out if whole else colp_out.at[0:4], slot if whole else slot.at[0:4], d)
        )
    for copy in third:
        copy.start()

    def squeeze(x):
        low = lax.broadcasted_iota(jnp.int32, (ROWS, 2 * COLS), 0) < 4
        return jnp.concatenate([x[:ROWS], jnp.where(low, x[ROWS : 2 * ROWS], x[2 * ROWS :])], axis=0)

    cu, cv = squeeze(count_u), squeeze(count_v)
    row16 = lax.broadcasted_iota(jnp.int32, (2 * ROWS, 2 * COLS), 0)
    row16 = (r * ROWS + jnp.where(row16 < 12, row16, row16 - 16)).astype(jnp.float32)
    fu = 0.5 + (row16 + 0.5) / total_rows
    fv = 0.5 + row16 / total_rows

    for copy in second:
        copy.wait_recv()
    col_u = jnp.where(inside, around(col_out[0], lambda d: col_in[d, 0]), 0.0)
    col_v = jnp.where(inside, around(col_out[1], lambda d: col_in[d, 1]), 0.0)
    elevation = around(elev_ref[...], lambda d: elev_in[d])
    load = jnp.where(
        inside, elevation + GRAVITY_DT * (east(col_u) - col_u + north(col_v) - col_v), 0.0
    )

    def operate(p):
        flow_u = depth_u * (p - west(p))
        flow_v = depth_v * (p - south(p))
        return p - GRAVITY_DT * (east(flow_u) - flow_u + north(flow_v) - flow_v)

    sub16 = lax.broadcasted_iota(jnp.int32, (16, COLS), 0)
    lane16 = lax.broadcasted_iota(jnp.int32, (16, COLS), 1)
    lane1 = lax.broadcasted_iota(jnp.int32, (1, COLS), 1)

    def dots(pairs):
        sums = jnp.zeros((16, COLS), jnp.float32)
        for m, (a, b) in enumerate(pairs):
            part = jnp.sum(a[:ROWS, :COLS] * b[:ROWS, :COLS], axis=0, keepdims=True)
            sums = jnp.where(sub16 == m, part, sums)
        sums = jnp.sum(sums, axis=1, keepdims=True)
        return jnp.sum(jnp.where(lane16 == sub16, sums, 0.0), axis=0, keepdims=True)

    def tx_copy(i, target, slot, sem):
        return pltpu.make_async_remote_copy(
            src_ref=mine.at[2 * i], dst_ref=tx_in.at[i, slot],
            send_sem=tx_send.at[i, sem], recv_sem=tx_recv.at[i, slot],
            device_id=(r, target), device_id_type=MESH,
        )

    def ty_copy(i, target, slot, sem):
        return pltpu.make_async_remote_copy(
            src_ref=mine.at[2 * i + 1], dst_ref=ty_in.at[i, slot],
            send_sem=ty_send.at[i, sem], recv_sem=ty_recv.at[i, slot],
            device_id=(target, c), device_id_type=MESH,
        )

    def spread(i, copy, me, n):
        def body(o, carry):
            copy(i, lax.rem(me + o, n), me, o).start()
            return carry

        lax.fori_loop(1, n, body, 0)

    def gather(i, copy, me, n):
        def body(o, carry):
            other = lax.rem(me + o, n)
            copy(i, other, other, o).wait_recv()
            return carry

        lax.fori_loop(1, n, body, 0)

    def drain(i, copy, me, n):
        def body(o, carry):
            copy(i, lax.rem(me + o, n), me, o).wait_send()
            return carry

        lax.fori_loop(1, n, body, 0)

    def total(i, row, cover_tx, cover_ty):
        mine[2 * i] = row
        spread(i, tx_copy, c, n_tx)
        tx_in[i, c] = row
        cover_tx()
        gather(i, tx_copy, c, n_tx)
        row = jnp.sum(tx_in[i], axis=0)
        mine[2 * i + 1] = row
        spread(i, ty_copy, r, n_ty)
        ty_in[i, r] = row
        cover_ty()
        gather(i, ty_copy, r, n_ty)
        return jnp.sum(ty_in[i], axis=0)

    def pick(row, m):
        return jnp.sum(jnp.where(lane1 == m, row, 0.0), axis=1, keepdims=True)

    def spread_out(px, pb, pv, qv, qc, qu):
        c1 = qc + north(qc)
        b1 = pb + south(pb)
        gu = 0.5 * (east(px) - west(px) + north(pv) - south(pv)) + 0.25 * (c1 + west(c1))
        gv = 0.5 * (north(qv) - south(qv) + east(qu) - west(qu)) + 0.25 * (b1 + east(b1))
        return gu[:ROWS, :COLS], gv[:ROWS, :COLS]

    inner = lax.rem(lane, 4) < 2
    low8 = sub < 4
    beside = jnp.where(inner, c, n_tx - 1 - c) > 0
    beyond = jnp.where(low8, n_ty - 1 - r, r) > 0

    def receive():
        for copy in third:
            copy.wait_recv()
        for f in range(6):
            side = jnp.where(inner, colp_in[COLUMN_SLOT[W], f], colp_in[COLUMN_SLOT[E], f])
            sides[f] = jnp.where(beside, side, 0.0)
        for f in range(4):
            upper = jnp.where(inner, colp_in[COLUMN_SLOT[NW], f], colp_in[COLUMN_SLOT[NE], f])
            lower = jnp.where(inner, colp_in[COLUMN_SLOT[SW], f], colp_in[COLUMN_SLOT[SE], f])
            corners[f] = jnp.where(beside & beyond, jnp.where(low8, upper, lower), 0.0)

    def prepare(k, carry):
        shift = lax.rem(126 - 4 * k + COLS, COLS)
        nb, sb = rown_in[k], rows_in[k]
        nb2, sb2 = rown2_in[k], rows2_in[k]

        def wide(f, ref, ends):
            side = pltpu.roll(sides[f], shift, 1)
            corner = pltpu.roll(corners[f], shift, 1) if f < 4 else side
            return tile(ref[k], side, jnp.where(beyond, ends, 0.0), corner)

        def both(f, ref):
            i = f - 2
            ends = jnp.where(
                low8,
                jnp.broadcast_to(nb2[i : i + 1], (ROWS, COLS)),
                jnp.broadcast_to(sb2[i : i + 1], (ROWS, COLS)),
            )
            return wide(f, ref, ends)

        u = wide(0, u_ref, jnp.where(low8, nb, sb))
        v = wide(1, v_ref, jnp.where(low8, turn(nb, -2, 0), turn(sb, 2, 0)))
        t = wide(4, t_ref, jnp.where(low8, turn(nb, 4, 0), turn(sb, 4, 0)))
        ts = wide(5, ts_ref, jnp.where(low8, turn(nb, 2, 0), turn(sb, -2, 0)))
        us = both(2, us_ref)
        vs = both(3, vs_ref)
        level = k.astype(jnp.float32)
        mask_u = jnp.where(cu > level, ADVECT, 0.0)
        mask_v = jnp.where(cv > level, ADVECT, 0.0)

        flux_x = mask_u * (ts - west(ts))
        flux_y = mask_v * (ts - south(ts))
        x, y = u * flux_x, v * flux_y
        xe, yn = east(x), north(y)
        gt = ts + (
            7.0 * (x + xe + y + yn) - (west(x) + east(xe) + south(y) + north(yn))
        ) * (1.0 / 12.0)
        gt_ref[k] = gt[:ROWS, :COLS]
        tw, tso = west(t), south(t)
        face_x = (7.0 * (t + tw) - (east(t) + west(tw))) * (1.0 / 12.0)
        face_y = (7.0 * (t + tso) - (north(t) + south(tso))) * (1.0 / 12.0)

        ue, vn = east(u), north(v)
        pair_v, pair_u = v + vn, u + ue
        v_bar = 0.25 * (pair_v + west(pair_v))
        u_bar = 0.25 * (pair_u + south(pair_u))
        kpu = mask_u * u
        kpv = mask_u * v_bar
        kb = mask_u * (fu - 0.5 * (north(u) - south(u)))
        kqv = mask_v * v
        kqu = mask_v * u_bar
        kc = -mask_v * (fv + 0.5 * (east(v) - west(v)))
        k_pu[k], k_pv[k], k_b[k] = kpu, kpv, kb
        k_qv[k], k_qu[k], k_c[k] = kqv, kqu, kc
        own_mu, own_mv = mask_u[:ROWS, :COLS], mask_v[:ROWS, :COLS]
        ku = -0.5 * own_mu * (ue - west(u))[:ROWS, :COLS]
        kv = -0.5 * own_mv * (vn - south(v))[:ROWS, :COLS]
        k_u[k] = ku + jnp.where(own_mu > 0.0, 1.0, 0.0)
        k_v[k] = kv + jnp.where(own_mv > 0.0, 1.0, 0.0)
        gu, gv = spread_out(kpu * us, kb * us, kpv * us, kqv * vs, kc * vs, kqu * vs)
        own_us, own_vs = us_ref[k], vs_ref[k]
        gu_ref[k] = gu + own_us + own_us * ku + (flux_x * face_x)[:ROWS, :COLS]
        gv_ref[k] = gv + own_vs + own_vs * kv + (flux_y * face_y)[:ROWS, :COLS]
        return carry

    third_of = levels // 3

    def cover_first():
        receive()
        lax.fori_loop(0, third_of, prepare, 0)

    p0 = load
    p1 = operate(p0)
    p2 = operate(p1)
    row = total(
        0, dots([(p0, p0), (p0, p1), (p1, p1), (p1, p2)]), lambda: None, cover_first
    )
    g00, g01, g11, g12 = [pick(row, m) for m in range(4)]
    alpha1 = g00 / g01
    norm1 = g00 - 2.0 * alpha1 * g01 + alpha1 * alpha1 * g11
    beta1 = norm1 / g00
    e0, e1 = 1.0 + beta1, -alpha1
    alpha2 = norm1 / (e0 * e0 * g01 + 2.0 * e0 * e1 * g11 + e1 * e1 * g12)
    d1 = e0 * p0 + e1 * p1
    x2 = alpha1 * p0 + alpha2 * d1
    w0 = (p0 - alpha1 * p1) - alpha2 * (e0 * p1 + e1 * p2)

    w1 = d1
    w2, w3 = operate(w0), operate(w1)
    w4, w5 = operate(w2), operate(w3)
    row = total(
        1,
        dots(
            [(w0, w0), (w0, w2), (w0, w3), (w1, w3), (w2, w2), (w2, w3), (w3, w3), (w2, w4), (w2, w5), (w3, w5)]
        ),
        lambda: lax.fori_loop(third_of, 2 * third_of, prepare, 0),
        lambda: lax.fori_loop(2 * third_of, levels, prepare, 0),
    )
    h00, h02, h03, h13, h22, h23, h33, h24, h25, h35 = [pick(row, m) for m in range(10)]
    beta2 = h00 / norm1
    twice, square = 2.0 * beta2, beta2 * beta2
    d_a_d = h02 + twice * h03 + square * h13
    ad_ad = h22 + twice * h23 + square * h33
    d_aaa_d = h24 + twice * h25 + square * h35
    r_a_d = h02 + beta2 * h03
    ar_ad = h22 + beta2 * h23
    alpha3 = h00 / d_a_d
    norm3 = h00 - 2.0 * alpha3 * r_a_d + alpha3 * alpha3 * ad_ad
    beta3 = norm3 / h00
    alpha4 = norm3 / (
        h02 + 2.0 * beta3 * r_a_d - 2.0 * alpha3 * ar_ad
        + beta3 * beta3 * d_a_d - 2.0 * alpha3 * beta3 * ad_ad + alpha3 * alpha3 * d_aaa_d
    )
    d2 = w0 + beta2 * w1
    d3 = w0 + beta3 * d2 - alpha3 * (w2 + beta2 * w3)
    answer = x2 + alpha3 * d2 + alpha4 * d3
    eta_ref[...] = answer[:ROWS, :COLS]
    slope_x = squeeze(answer - west(answer))
    slope_y = squeeze(answer - south(answer))

    def finish(k, carry):
        thick = 1.0 + k.astype(jnp.float32) * (1.0 / levels)
        dx, dy = thick * slope_x, thick * slope_y
        gu, gv = spread_out(k_pu[k] * dx, k_b[k] * dx, k_pv[k] * dx, k_qv[k] * dy, k_c[k] * dy, k_qu[k] * dy)
        gu_ref[k] = gu_ref[k] + gu + k_u[k] * dx[:ROWS, :COLS]
        gv_ref[k] = gv_ref[k] + gv + k_v[k] * dy[:ROWS, :COLS]
        return carry

    lax.fori_loop(0, levels, finish, 0)

    for copy in first + second + third:
        copy.wait_send()
    for i in range(2):
        drain(i, tx_copy, c, n_tx)
        drain(i, ty_copy, r, n_ty)


def on_device(n_ty, n_tx, u, v, t, count, us, vs, ts, elevation):
    levels = u.shape[0]
    block = jax.ShapeDtypeStruct(u.shape, jnp.float32)
    f32 = jnp.float32
    wide = pltpu.VMEM((levels, 2 * ROWS, 2 * COLS), f32)
    own = pltpu.VMEM((levels, ROWS, COLS), f32)
    two = pltpu.VMEM((levels, 2, COLS), f32)
    return pl.pallas_call(
        functools.partial(kernel, levels, n_ty, n_tx),
        out_shape=(block, block, block, jax.ShapeDtypeStruct(elevation.shape, f32)),
        in_specs=[pl.BlockSpec(memory_space=pltpu.VMEM)] * 8,
        out_specs=[pl.BlockSpec(memory_space=pltpu.VMEM)] * 4,
        scratch_shapes=[
            pltpu.VMEM((8, ROWS, COLS), jnp.int32),
            pltpu.VMEM((8, ROWS, COLS), f32),
            pltpu.VMEM((2, ROWS, COLS), f32),
            pltpu.VMEM((8, 2, ROWS, COLS), f32),
            pltpu.VMEM((6, ROWS, COLS), f32),
            pltpu.VMEM((6, 6, ROWS, COLS), f32),
            own, own, two, two,
            own, own, two, two,
            pltpu.VMEM((6, ROWS, COLS), f32),
            pltpu.VMEM((4, ROWS, COLS), f32),
            pltpu.VMEM((4, 1, COLS), f32),
            pltpu.VMEM((2, n_tx, 1, COLS), f32),
            pltpu.VMEM((2, n_ty, 1, COLS), f32),
            wide, wide, wide, wide, wide, wide, own, own,
            pltpu.SemaphoreType.DMA((34,)),
            pltpu.SemaphoreType.DMA((34,)),
            pltpu.SemaphoreType.DMA((2, n_tx)),
            pltpu.SemaphoreType.DMA((2, n_tx)),
            pltpu.SemaphoreType.DMA((2, n_ty)),
            pltpu.SemaphoreType.DMA((2, n_ty)),
        ],
        compiler_params=pltpu.CompilerParams(
            collective_id=0, has_side_effects=True, vmem_limit_bytes=32 * 1024 * 1024
        ),
    )(u, v, t, count, us, vs, ts, elevation)


def solution(mesh):
    field, surface = P(None, "ty", "tx"), P("ty", "tx")
    return jax.shard_map(
        functools.partial(on_device, mesh.shape["ty"], mesh.shape["tx"]),
        mesh=mesh,
        in_specs=(field, field, field, surface, field, field, field, surface),
        out_specs=(field, field, field, surface),
        check_vma=False,
    )
```

time: 887 us -> 63.7 us (0.07)
  blocking collectives: 692 us -> 0 us
  starting transfers between devices: 85.9 us -> 0 us
  Pallas kernels: 0 us -> 53.4 us
  waiting for transfers between devices: 50 us -> 0 us
  other arithmetic: 28.9 us -> 0 us
  between operations: 10.9 us -> 0.66 us
    psum x7 -> x0, blocking collectives: 692 us -> none  [the longest x4 391 us: squares(): return lax.psum(jnp.sum(residual * residual), ('ty', 'tx'))]
    ppermute x32 -> x0, starting transfers between devices: 85.9 us -> none  [the longest x16 56.4 us: padded(): before = lax.ppermute(last, axis, up)]
    pallas_call x0 -> x1, Pallas kernels: none -> 53.4 us  [on_device(): pl.pallas_call(functools.partial(kernel, levels, n_ty, n_tx), out_shape=(...]
    ppermute x32 -> x0, waiting for transfers between devices: 50 us -> none  [the longest x16 47 us: padded(): after = lax.ppermute(first, axis, down)]
  transfers between devices with their start and end apart: 32 -> 0, of which waited for: 17 -> 0; matrix products, arithmetic and copies ran while one was open for 0% -> 0% of each run, Pallas kernels for 0% -> 0%
where the time goes in v1:
time: 63.7 us; the launch traced here: 63.3 us
  Pallas kernels  53.4 us (84%)
  local copies, waits for them, and re-layouts  9.31 us (15%)
  between operations  0.66 us (1%)
    pallas_call x1, Pallas kernels, on_device(): pl.pallas_call(functools.partial(kernel, levels, n_ty, n_tx), out_shape=(...  53.4 us
    unnamed x20, local copies, waits for them, and re-layouts  9.31 us

profile of v1, /device:TPU:1, one launch (start us, length us, event | category | flops | bytes accessed | tf_op | source)
XLA Modules:
  0.0 63.3 jit_solution(38697794869667875)
XLA Ops:
  0.6 0.0 copy-start
  0.6 0.9 %copy-done = f32[30,8,128]{2,1,0:T(8,128)S(1)} copy-done((f32[30,8,128]{2,1,0:T(8,128)S(1)}, f32[30,8,128]{2,1,0:T(8,128)}, u32[]{:S(2)}) %copy-start) | copy-done | bytes 122904
  1.5 0.0 copy-start.1
  1.5 0.9 %copy-done.1 = f32[30,8,128]{2,1,0:T(8,128)S(1)} copy-done((f32[30,8,128]{2,1,0:T(8,128)S(1)}, f32[30,8,128]{2,1,0:T(8,128)}, u32[]{:S(2)}) %copy-start.1) | copy-done | bytes 122904
  2.4 0.0 copy-start.2
  2.4 0.9 %copy-done.2 = f32[30,8,128]{2,1,0:T(8,128)S(1)} copy-done((f32[30,8,128]{2,1,0:T(8,128)S(1)}, f32[30,8,128]{2,1,0:T(8,128)}, u32[]{:S(2)}) %copy-start.2) | copy-done | bytes 122904
  3.3 0.0 copy-start.3
  3.3 0.9 %copy-done.3 = f32[30,8,128]{2,1,0:T(8,128)S(1)} copy-done((f32[30,8,128]{2,1,0:T(8,128)S(1)}, f32[30,8,128]{2,1,0:T(8,128)}, u32[]{:S(2)}) %copy-start.3) | copy-done | bytes 122904
  4.2 0.0 copy-start.4
  4.2 0.9 %copy-done.4 = f32[30,8,128]{2,1,0:T(8,128)S(1)} copy-done((f32[30,8,128]{2,1,0:T(8,128)S(1)}, f32[30,8,128]{2,1,0:T(8,128)}, u32[]{:S(2)}) %copy-start.4) | copy-done | bytes 122904
  5.1 0.0 copy-start.5
  5.1 0.9 %copy-done.5 = f32[30,8,128]{2,1,0:T(8,128)S(1)} copy-done((f32[30,8,128]{2,1,0:T(8,128)S(1)}, f32[30,8,128]{2,1,0:T(8,128)}, u32[]{:S(2)}) %copy-start.5) | copy-done | bytes 122904
  6.0 0.0 copy-start.6
  6.0 0.7 %copy-done.6 = s32[8,128]{1,0:T(8,128)S(1)} copy-done((s32[8,128]{1,0:T(8,128)S(1)}, s32[8,128]{1,0:T(8,128)}, u32[]{:S(2)}) %copy-start.6) | copy-done | bytes 4120
  6.7 0.0 copy-start.7
  6.7 0.7 %copy-done.7 = f32[8,128]{1,0:T(8,128)S(1)} copy-done((f32[8,128]{1,0:T(8,128)S(1)}, f32[8,128]{1,0:T(8,128)}, u32[]{:S(2)}) %copy-start.7) | copy-done | bytes 4120
  7.4 53.4 %shard_map.111 = (f32[30,8,128]{2,1,0:T(8,128)S(1)}, f32[30,8,128]{2,1,0:T(8,128)S(1)}, f32[30,8,128]{2,1,0:T(8,128)S(1)}, f32[8,128]{1,0:T(8,128)S(1)}) custom-call(f32[30,8,128]{2,1,0:T(8,128)S(1)} %copy-done, f32[30,8,128]{2,1,0:T(8,128)S(1)} %copy-done.1, f32[30,8,128]{2,1,0:T(8,128)S(1)} %copy-done.2, s32[8,128]{1,0:T(8,128)S(1)} %copy-done.6, ...), custom_call_target="tpu_custom_call" | custom-call | tf_op jit(solution)/shard_map/pallas_call | solution.py:418
  60.8 0.7 %copy.16 = f32[30,8,128]{2,1,0:T(8,128)} copy(f32[30,8,128]{2,1,0:T(8,128)S(1)} %get-tuple-element.8) | data formatting | bytes 245760
  61.5 0.6 %copy.17 = f32[30,8,128]{2,1,0:T(8,128)} copy(f32[30,8,128]{2,1,0:T(8,128)S(1)} %get-tuple-element.9) | data formatting | bytes 245760
  62.1 0.6 %copy.18 = f32[30,8,128]{2,1,0:T(8,128)} copy(f32[30,8,128]{2,1,0:T(8,128)S(1)} %get-tuple-element.10) | data formatting | bytes 245760
  62.8 0.6 copy.19
Async XLA Ops:
  0.6 0.9 %copy-start = (f32[30,8,128]{2,1,0:T(8,128)S(1)}, f32[30,8,128]{2,1,0:T(8,128)}, u32[]{:S(2)}) copy-start(f32[30,8,128]{2,1,0:T(8,128)} %u_ref.1) | copy-start | bytes 368644
  1.5 0.9 %copy-start.1 = (f32[30,8,128]{2,1,0:T(8,128)S(1)}, f32[30,8,128]{2,1,0:T(8,128)}, u32[]{:S(2)}) copy-start(f32[30,8,128]{2,1,0:T(8,128)} %v_ref.1) | copy-start | bytes 368644
  2.4 0.9 %copy-start.2 = (f32[30,8,128]{2,1,0:T(8,128)S(1)}, f32[30,8,128]{2,1,0:T(8,128)}, u32[]{:S(2)}) copy-start(f32[30,8,128]{2,1,0:T(8,128)} %t_ref.1) | copy-start | bytes 368644
  3.3 0.9 %copy-start.3 = (f32[30,8,128]{2,1,0:T(8,128)S(1)}, f32[30,8,128]{2,1,0:T(8,128)}, u32[]{:S(2)}) copy-start(f32[30,8,128]{2,1,0:T(8,128)} %us_ref.1) | copy-start | bytes 368644
  4.2 0.9 %copy-start.4 = (f32[30,8,128]{2,1,0:T(8,128)S(1)}, f32[30,8,128]{2,1,0:T(8,128)}, u32[]{:S(2)}) copy-start(f32[30,8,128]{2,1,0:T(8,128)} %vs_ref.1) | copy-start | bytes 368644
  5.1 0.9 %copy-start.5 = (f32[30,8,128]{2,1,0:T(8,128)S(1)}, f32[30,8,128]{2,1,0:T(8,128)}, u32[]{:S(2)}) copy-start(f32[30,8,128]{2,1,0:T(8,128)} %ts_ref.1) | copy-start | bytes 368644
  6.0 0.7 %copy-start.6 = (s32[8,128]{1,0:T(8,128)S(1)}, s32[8,128]{1,0:T(8,128)}, u32[]{:S(2)}) copy-start(s32[8,128]{1,0:T(8,128)} %count_ref.1) | copy-start | bytes 12292
  6.7 0.7 %copy-start.7 = (f32[8,128]{1,0:T(8,128)S(1)}, f32[8,128]{1,0:T(8,128)}, u32[]{:S(2)}) copy-start(f32[8,128]{1,0:T(8,128)} %elev_ref.1) | copy-start | bytes 12292

commit v2 on v1

--- a/solution.py
+++ b/solution.py
@@ -15,8 +15,6 @@
 E, W, N, S, NE, NW, SE, SW = range(8)
 WAY = ((0, 1), (0, -1), (1, 0), (-1, 0), (1, 1), (1, -1), (-1, 1), (-1, -1))
 OPPOSITE = (W, E, S, N, SW, SE, NW, NE)
-COLUMN_SLOT = {E: 0, W: 1, NE: 2, NW: 3, SE: 4, SW: 5}
-
 
 def turn(x, shift, axis):
     return pltpu.roll(x, shift % x.shape[axis], axis)
@@ -44,16 +42,24 @@
     )
 
 
+def spread_out(px, pb, pv, qv, qc, qu):
+    c1 = qc + north(qc)
+    b1 = pb + south(pb)
+    gu = 0.5 * (east(px) - west(px) + north(pv) - south(pv)) + 0.25 * (c1 + west(c1))
+    gv = 0.5 * (north(qv) - south(qv) + east(qu) - west(qu)) + 0.25 * (b1 + east(b1))
+    return gu[:ROWS, :COLS], gv[:ROWS, :COLS]
+
+
 def kernel(
     levels, n_ty, n_tx,
-    u_ref, v_ref, t_ref, count_ref, us_ref, vs_ref, ts_ref, elev_ref,
-    gu_ref, gv_ref, gt_ref, eta_ref,
+    u_hbm, v_hbm, t_hbm, count_hbm, us_hbm, vs_hbm, ts_hbm, elev_hbm,
+    gu_ref, gv_ref, gt_ref, eta_ref, slope_ref,
+    k_pu, k_pv, k_b, k_qv, k_qu, k_c, k_u, k_v,
+    u_ref, v_ref, t_ref, us_ref, vs_ref, ts_ref, count_ref, elev_ref,
     count_in, elev_in, col_out, col_in,
-    colp_out, colp_in, rown_out, rows_out, rown2_out, rows2_out,
-    rown_in, rows_in, rown2_in, rows2_in,
+    colp_out, colp_in, corner_in, rown_out, rows_out, rown2_out, rows2_out, row_in, row2_in,
     sides, corners, mine, tx_in, ty_in,
-    k_pu, k_pv, k_b, k_qv, k_qu, k_c, k_u, k_v,
-    hop_send, hop_recv, tx_send, tx_recv, ty_send, ty_recv,
+    load_sem, send_sem, recv_sem,
 ):
     r, c = lax.axis_index("ty"), lax.axis_index("tx")
     total_rows = ROWS * n_ty
@@ -65,28 +71,41 @@
     def hop(number, src, dst, d):
         return pltpu.make_async_remote_copy(
             src_ref=src, dst_ref=dst,
-            send_sem=hop_send.at[number], recv_sem=hop_recv.at[number],
+            send_sem=send_sem.at[number], recv_sem=recv_sem.at[number],
             device_id=at(d), device_id_type=MESH,
         )
 
+    def whole(number, ref):
+        return hop(number, ref, ref, E)
+
+    def fetch(i, src, dst):
+        copy = pltpu.make_async_copy(src, dst, load_sem.at[i])
+        copy.start()
+        return copy
+
+    fetches = [
+        fetch(0, u_hbm, u_ref), fetch(1, v_hbm, v_ref), fetch(2, us_hbm, us_ref), fetch(3, vs_hbm, vs_ref),
+        fetch(4, t_hbm, t_ref), fetch(5, ts_hbm, ts_ref), fetch(6, count_hbm, count_ref),
+        fetch(7, elev_hbm, elev_ref),
+    ]
+    tx_order = sorted(range(1, n_tx), key=lambda o: -min(o, n_tx - o))
+    ty_order = sorted(range(1, n_ty), key=lambda o: -(min(o % 8, 8 - o % 8) + min(o // 8, n_ty // 8 - o // 8)))
+
     barrier = pltpu.get_barrier_semaphore()
 
-    def greet_tx(o, carry):
+    for o in ty_order:
+        pl.semaphore_signal(barrier, inc=1, device_id=(lax.rem(r + o, n_ty), c), device_id_type=MESH)
+    for o in tx_order:
         pl.semaphore_signal(barrier, inc=1, device_id=(r, lax.rem(c + o, n_tx)), device_id_type=MESH)
-        return carry
-
-    def greet_ty(o, carry):
-        pl.semaphore_signal(barrier, inc=1, device_id=(lax.rem(r + o, n_ty), c), device_id_type=MESH)
-        return carry
-
-    lax.fori_loop(1, n_ty, greet_ty, 0)
-    lax.fori_loop(1, n_tx, greet_tx, 0)
     for d in (NE, NW, SE, SW):
         pl.semaphore_signal(barrier, inc=1, device_id=at(d), device_id_type=MESH)
 
     lane = lax.broadcasted_iota(jnp.int32, (ROWS, COLS), 1)
     sub = lax.broadcasted_iota(jnp.int32, (ROWS, COLS), 0)
     fields = (u_ref, v_ref, us_ref, vs_ref, t_ref, ts_ref)
+
+    for copy in fetches:
+        copy.wait()
 
     def pack(k, packed):
         x = [f[k] for f in fields]
@@ -110,10 +129,9 @@
 
     pl.semaphore_wait(barrier, (n_tx - 1) + (n_ty - 1) + 4)
 
-    first = [hop(d, count_ref, count_in.at[OPPOSITE[d]], d) for d in range(8)]
-    first += [hop(8 + d, elev_ref, elev_in.at[OPPOSITE[d]], d) for d in range(8)]
-    for copy in first:
-        copy.start()
+    for d in range(8):
+        hop(0, count_ref, count_in.at[OPPOSITE[d]], d).start()
+        hop(1, elev_ref, elev_in.at[OPPOSITE[d]], d).start()
 
     wide_row = lax.broadcasted_iota(jnp.int32, (3 * ROWS, 2 * COLS), 0)
     wide_col = lax.broadcasted_iota(jnp.int32, (3 * ROWS, 2 * COLS), 1)
@@ -127,8 +145,8 @@
             [jnp.concatenate([a, b], axis=1) for a, b in zip((own, part(N), part(S)), rim)], axis=0
         )
 
-    for copy in first:
-        copy.wait_recv()
+    whole(0, count_in).wait_recv()
+    whole(1, elev_in).wait_recv()
     count = jnp.where(inside, around(count_ref[...], lambda d: count_in[d]).astype(jnp.float32), 0.0)
     count_u = jnp.minimum(count, west(count))
     count_v = jnp.minimum(count, south(count))
@@ -143,22 +161,17 @@
         col_v = col_v + jnp.where(own_v > float(k), vs_ref[k], 0.0)
     col_out[0] = col_u
     col_out[1] = col_v
-    second = [hop(16 + d, col_out, col_in.at[OPPOSITE[d]], d) for d in range(8)]
-    for copy in second:
-        copy.start()
-
-    third = [
-        hop(24, rown_out, rows_in, N), hop(25, rows_out, rown_in, S),
-        hop(26, rown2_out, rows2_in, N), hop(27, rows2_out, rown2_in, S),
-    ]
-    for i, d in enumerate((E, W, NE, NW, SE, SW)):
-        slot = colp_in.at[COLUMN_SLOT[OPPOSITE[d]]]
-        whole = d in (E, W)
-        third.append(
-            hop(28 + i, colp_out if whole else colp_out.at[0:4], slot if whole else slot.at[0:4], d)
-        )
-    for copy in third:
-        copy.start()
+    for d in range(8):
+        hop(2, col_out, col_in.at[OPPOSITE[d]], d).start()
+
+    hop(3, rown_out, row_in.at[1], N).start()
+    hop(3, rows_out, row_in.at[0], S).start()
+    hop(4, rown2_out, row2_in.at[1], N).start()
+    hop(4, rows2_out, row2_in.at[0], S).start()
+    for d in (E, W):
+        hop(5, colp_out, colp_in.at[OPPOSITE[d]], d).start()
+    for d in (NE, NW, SE, SW):
+        hop(6, colp_out.at[0:4], corner_in.at[OPPOSITE[d] - NE], d).start()
 
     def squeeze(x):
         low = lax.broadcasted_iota(jnp.int32, (ROWS, 2 * COLS), 0) < 4
@@ -170,8 +183,7 @@
     fu = 0.5 + (row16 + 0.5) / total_rows
     fv = 0.5 + row16 / total_rows
 
-    for copy in second:
-        copy.wait_recv()
+    whole(2, col_in).wait_recv()
     col_u = jnp.where(inside, around(col_out[0], lambda d: col_in[d, 0]), 0.0)
     col_v = jnp.where(inside, around(col_out[1], lambda d: col_in[d, 1]), 0.0)
     elevation = around(elev_ref[...], lambda d: elev_in[d])
@@ -196,65 +208,36 @@
         sums = jnp.sum(sums, axis=1, keepdims=True)
         return jnp.sum(jnp.where(lane16 == sub16, sums, 0.0), axis=0, keepdims=True)
 
-    def tx_copy(i, target, slot, sem):
+    def tx_copy(i, o):
         return pltpu.make_async_remote_copy(
-            src_ref=mine.at[2 * i], dst_ref=tx_in.at[i, slot],
-            send_sem=tx_send.at[i, sem], recv_sem=tx_recv.at[i, slot],
-            device_id=(r, target), device_id_type=MESH,
-        )
-
-    def ty_copy(i, target, slot, sem):
+            src_ref=mine.at[2 * i], dst_ref=tx_in.at[i, o - 1],
+            send_sem=send_sem.at[7 + i], recv_sem=recv_sem.at[7 + i],
+            device_id=(r, lax.rem(c + o, n_tx)), device_id_type=MESH,
+        )
+
+    def ty_copy(i, o):
         return pltpu.make_async_remote_copy(
-            src_ref=mine.at[2 * i + 1], dst_ref=ty_in.at[i, slot],
-            send_sem=ty_send.at[i, sem], recv_sem=ty_recv.at[i, slot],
-            device_id=(target, c), device_id_type=MESH,
-        )
-
-    def spread(i, copy, me, n):
-        def body(o, carry):
-            copy(i, lax.rem(me + o, n), me, o).start()
-            return carry
-
-        lax.fori_loop(1, n, body, 0)
-
-    def gather(i, copy, me, n):
-        def body(o, carry):
-            other = lax.rem(me + o, n)
-            copy(i, other, other, o).wait_recv()
-            return carry
-
-        lax.fori_loop(1, n, body, 0)
-
-    def drain(i, copy, me, n):
-        def body(o, carry):
-            copy(i, lax.rem(me + o, n), me, o).wait_send()
-            return carry
-
-        lax.fori_loop(1, n, body, 0)
+            src_ref=mine.at[2 * i + 1], dst_ref=ty_in.at[i, o - 1],
+            send_sem=send_sem.at[9 + i], recv_sem=recv_sem.at[9 + i],
+            device_id=(lax.rem(r + o, n_ty), c), device_id_type=MESH,
+        )
 
     def total(i, row, cover_tx, cover_ty):
         mine[2 * i] = row
-        spread(i, tx_copy, c, n_tx)
-        tx_in[i, c] = row
+        for o in tx_order:
+            tx_copy(i, o).start()
         cover_tx()
-        gather(i, tx_copy, c, n_tx)
-        row = jnp.sum(tx_in[i], axis=0)
+        whole(7 + i, tx_in.at[i]).wait_recv()
+        row = row + jnp.sum(tx_in[i], axis=0)
         mine[2 * i + 1] = row
-        spread(i, ty_copy, r, n_ty)
-        ty_in[i, r] = row
+        for o in ty_order:
+            ty_copy(i, o).start()
         cover_ty()
-        gather(i, ty_copy, r, n_ty)
-        return jnp.sum(ty_in[i], axis=0)
+        whole(9 + i, ty_in.at[i]).wait_recv()
+        return row + jnp.sum(ty_in[i], axis=0)
 
     def pick(row, m):
         return jnp.sum(jnp.where(lane1 == m, row, 0.0), axis=1, keepdims=True)
-
-    def spread_out(px, pb, pv, qv, qc, qu):
-        c1 = qc + north(qc)
-        b1 = pb + south(pb)
-        gu = 0.5 * (east(px) - west(px) + north(pv) - south(pv)) + 0.25 * (c1 + west(c1))
-        gv = 0.5 * (north(qv) - south(qv) + east(qu) - west(qu)) + 0.25 * (b1 + east(b1))
-        return gu[:ROWS, :COLS], gv[:ROWS, :COLS]
 
     inner = lax.rem(lane, 4) < 2
     low8 = sub < 4
@@ -262,20 +245,20 @@
     beyond = jnp.where(low8, n_ty - 1 - r, r) > 0
 
     def receive():
-        for copy in third:
-            copy.wait_recv()
+        for number, ref in ((3, row_in), (4, row2_in), (5, colp_in), (6, corner_in)):
+            whole(number, ref).wait_recv()
         for f in range(6):
-            side = jnp.where(inner, colp_in[COLUMN_SLOT[W], f], colp_in[COLUMN_SLOT[E], f])
+            side = jnp.where(inner, colp_in[W, f], colp_in[E, f])
             sides[f] = jnp.where(beside, side, 0.0)
         for f in range(4):
-            upper = jnp.where(inner, colp_in[COLUMN_SLOT[NW], f], colp_in[COLUMN_SLOT[NE], f])
-            lower = jnp.where(inner, colp_in[COLUMN_SLOT[SW], f], colp_in[COLUMN_SLOT[SE], f])
+            upper = jnp.where(inner, corner_in[NW - NE, f], corner_in[NE - NE, f])
+            lower = jnp.where(inner, corner_in[SW - NE, f], corner_in[SE - NE, f])
             corners[f] = jnp.where(beside & beyond, jnp.where(low8, upper, lower), 0.0)
 
     def prepare(k, carry):
         shift = lax.rem(126 - 4 * k + COLS, COLS)
-        nb, sb = rown_in[k], rows_in[k]
-        nb2, sb2 = rown2_in[k], rows2_in[k]
+        nb, sb = row_in[0, k], row_in[1, k]
+        nb2, sb2 = row2_in[0, k], row2_in[1, k]
 
         def wide(f, ref, ends):
             side = pltpu.roll(sides[f], shift, 1)
@@ -388,64 +371,92 @@
     d3 = w0 + beta3 * d2 - alpha3 * (w2 + beta2 * w3)
     answer = x2 + alpha3 * d2 + alpha4 * d3
     eta_ref[...] = answer[:ROWS, :COLS]
-    slope_x = squeeze(answer - west(answer))
-    slope_y = squeeze(answer - south(answer))
-
-    def finish(k, carry):
+    slope_ref[0] = squeeze(answer - west(answer))
+    slope_ref[1] = squeeze(answer - south(answer))
+
+    for number, ref in (
+        (0, count_in), (1, elev_in), (2, col_in), (3, row_in), (4, row2_in), (5, colp_in), (6, corner_in),
+        (7, tx_in.at[0]), (8, tx_in.at[1]), (9, ty_in.at[0]), (10, ty_in.at[1]),
+    ):
+        whole(number, ref).wait_send()
+
+
+def finish(
+    levels, pieces,
+    gu_ref, gv_ref, gt_ref, eta_ref, slope_ref, k_pu, k_pv, k_b, k_qv, k_qu, k_c, k_u, k_v,
+    gu_hbm, gv_hbm, gt_hbm, eta_hbm,
+    gu_out, gv_out, sems,
+):
+    copies = [
+        pltpu.make_async_copy(gt_ref, gt_hbm, sems.at[0]),
+        pltpu.make_async_copy(eta_ref, eta_hbm, sems.at[1]),
+    ]
+    for copy in copies:
+        copy.start()
+    slope_x, slope_y = slope_ref[0], slope_ref[1]
+
+    def level(k, carry):
         thick = 1.0 + k.astype(jnp.float32) * (1.0 / levels)
         dx, dy = thick * slope_x, thick * slope_y
         gu, gv = spread_out(k_pu[k] * dx, k_b[k] * dx, k_pv[k] * dx, k_qv[k] * dy, k_c[k] * dy, k_qu[k] * dy)
-        gu_ref[k] = gu_ref[k] + gu + k_u[k] * dx[:ROWS, :COLS]
-        gv_ref[k] = gv_ref[k] + gv + k_v[k] * dy[:ROWS, :COLS]
+        gu_out[k] = gu_ref[k] + gu + k_u[k] * dx[:ROWS, :COLS]
+        gv_out[k] = gv_ref[k] + gv + k_v[k] * dy[:ROWS, :COLS]
         return carry
 
-    lax.fori_loop(0, levels, finish, 0)
-
-    for copy in first + second + third:
-        copy.wait_send()
-    for i in range(2):
-        drain(i, tx_copy, c, n_tx)
-        drain(i, ty_copy, r, n_ty)
+    size = levels // pieces
+    for i in range(pieces):
+        lax.fori_loop(i * size, (i + 1) * size, level, 0)
+        part = pl.ds(i * size, size)
+        for g, (src, dst) in enumerate(((gu_out, gu_hbm), (gv_out, gv_hbm))):
+            copy = pltpu.make_async_copy(src.at[part], dst.at[part], sems.at[2 + 2 * i + g])
+            copy.start()
+            copies.append(copy)
+    for copy in copies:
+        copy.wait()
 
 
 def on_device(n_ty, n_tx, u, v, t, count, us, vs, ts, elevation):
     levels = u.shape[0]
-    block = jax.ShapeDtypeStruct(u.shape, jnp.float32)
     f32 = jnp.float32
-    wide = pltpu.VMEM((levels, 2 * ROWS, 2 * COLS), f32)
+    block = jax.ShapeDtypeStruct(u.shape, f32)
+    face = jax.ShapeDtypeStruct(elevation.shape, f32)
+    around = jax.ShapeDtypeStruct((levels, 2 * ROWS, 2 * COLS), f32)
+    slopes = jax.ShapeDtypeStruct((2, 2 * ROWS, 2 * COLS), f32)
     own = pltpu.VMEM((levels, ROWS, COLS), f32)
     two = pltpu.VMEM((levels, 2, COLS), f32)
-    return pl.pallas_call(
+    tiles = lambda *n, dtype=f32: pltpu.VMEM((*n, ROWS, COLS), dtype)
+    vmem, hbm = pl.BlockSpec(memory_space=pltpu.VMEM), pl.BlockSpec(memory_space=pltpu.HBM)
+    parts = pl.pallas_call(
         functools.partial(kernel, levels, n_ty, n_tx),
-        out_shape=(block, block, block, jax.ShapeDtypeStruct(elevation.shape, f32)),
-        in_specs=[pl.BlockSpec(memory_space=pltpu.VMEM)] * 8,
-        out_specs=[pl.BlockSpec(memory_space=pltpu.VMEM)] * 4,
+        out_shape=(block, block, block, face, slopes) + (around,) * 6 + (block, block),
+        in_specs=[hbm] * 8,
+        out_specs=[vmem] * 13,
         scratch_shapes=[
-            pltpu.VMEM((8, ROWS, COLS), jnp.int32),
-            pltpu.VMEM((8, ROWS, COLS), f32),
-            pltpu.VMEM((2, ROWS, COLS), f32),
-            pltpu.VMEM((8, 2, ROWS, COLS), f32),
-            pltpu.VMEM((6, ROWS, COLS), f32),
-            pltpu.VMEM((6, 6, ROWS, COLS), f32),
-            own, own, two, two,
-            own, own, two, two,
-            pltpu.VMEM((6, ROWS, COLS), f32),
-            pltpu.VMEM((4, ROWS, COLS), f32),
+            own, own, own, own, own, own, tiles(dtype=jnp.int32), tiles(),
+            tiles(8, dtype=jnp.int32), tiles(8), tiles(2), tiles(8, 2),
+            tiles(6), tiles(2, 6), tiles(4, 4), own, own, two, two,
+            tiles(2, levels), pltpu.VMEM((2, levels, 2, COLS), f32),
+            tiles(6), tiles(4),
             pltpu.VMEM((4, 1, COLS), f32),
-            pltpu.VMEM((2, n_tx, 1, COLS), f32),
-            pltpu.VMEM((2, n_ty, 1, COLS), f32),
-            wide, wide, wide, wide, wide, wide, own, own,
-            pltpu.SemaphoreType.DMA((34,)),
-            pltpu.SemaphoreType.DMA((34,)),
-            pltpu.SemaphoreType.DMA((2, n_tx)),
-            pltpu.SemaphoreType.DMA((2, n_tx)),
-            pltpu.SemaphoreType.DMA((2, n_ty)),
-            pltpu.SemaphoreType.DMA((2, n_ty)),
+            pltpu.VMEM((2, n_tx - 1, 1, COLS), f32),
+            pltpu.VMEM((2, n_ty - 1, 1, COLS), f32),
+            pltpu.SemaphoreType.DMA((8,)),
+            pltpu.SemaphoreType.DMA((11,)),
+            pltpu.SemaphoreType.DMA((11,)),
         ],
         compiler_params=pltpu.CompilerParams(
             collective_id=0, has_side_effects=True, vmem_limit_bytes=32 * 1024 * 1024
         ),
-    )(u, v, t, count, us, vs, ts, elevation)
+    )(*[pltpu.with_memory_space_constraint(x, pltpu.HBM) for x in (u, v, t, count, us, vs, ts, elevation)])
+    pieces = 3
+    return pl.pallas_call(
+        functools.partial(finish, levels, pieces),
+        out_shape=(block, block, block, face),
+        in_specs=[vmem] * 13,
+        out_specs=[hbm] * 4,
+        scratch_shapes=[own, own, pltpu.SemaphoreType.DMA((2 + 2 * pieces,))],
+        compiler_params=pltpu.CompilerParams(vmem_limit_bytes=16 * 1024 * 1024),
+    )(*parts)
 
 
 def solution(mesh):

time: 63.7 us -> 51.1 us (0.80)
  local copies, waits for them, and re-layouts: 9.31 us -> 0 us
  Pallas kernels: 53.4 us -> 50.3 us
    unnamed x20 -> x0, local copies, waits for them, and re-layouts: 9.31 us -> none
    pallas_call x1, Pallas kernels: 53.4 us -> 46.9 us  [on_device(): pl.pallas_call(functools.partial(kernel, levels, n_ty, n_tx), out_shape=(...]
    pallas_call x0 -> x1, Pallas kernels: none -> 3.38 us  [on_device(): pl.pallas_call(functools.partial(finish, levels, pieces), out_shape=(bloc...]
where the time goes in v2:
time: 51.1 us; the launch traced here: 50.9 us
  Pallas kernels  50.3 us (98%)
  between operations  0.64 us (1%)
    pallas_call x1, Pallas kernels, on_device(): pl.pallas_call(functools.partial(kernel, levels, n_ty, n_tx), out_shape=(...  46.9 us
    pallas_call x1, Pallas kernels, on_device(): pl.pallas_call(functools.partial(finish, levels, pieces), out_shape=(bloc...  3.38 us

profile of v2, /device:TPU:1, one launch (start us, length us, event | category | flops | bytes accessed | tf_op | source)
XLA Modules:
  0.0 50.9 jit_solution(4046105346930206236)
XLA Ops:
  0.6 46.9 %shard_map.111 = (f32[30,8,128]{2,1,0:T(8,128)S(1)}, f32[30,8,128]{2,1,0:T(8,128)S(1)}, f32[30,8,128]{2,1,0:T(8,128)S(1)}, f32[8,128]{1,0:T(8,128)S(1)}, f32[2,1...) custom-call(f32[30,8,128]{2,1,0:T(8,128)} %u_hbm.1, ...), custom_call_target="tpu_custom_call" | custom-call | tf_op jit(solution)/shard_map/pallas_call | solution.py:429
  47.6 3.4 %shard_map.112 = (f32[30,8,128]{2,1,0:T(8,128)}, f32[30,8,128]{2,1,0:T(8,128)}, f32[30,8,128]{2,1,0:T(8,128)}, f32[8,128]{1,0:T(8,128)}) custom-call(f32[30,8,128]{2,1,0:T(8,128)S(1)} %get-tuple-element.17.gu_ref, f32[30,8,128]{2,1,0:T(8,128)S(1)} %get-tuple-element.18.gv_ref, f32[30,8,128]{2,1,0:T(8,128)S(1)} %get-tuple-element.19.gt_ref, ...), custom_call_target="tpu_custom_call" | custom-call | tf_op jit(solution)/shard_map/pallas_call | solution.py:452

commit v3 on v2

--- a/solution.py
+++ b/solution.py
@@ -12,9 +12,10 @@
 GRAVITY_DT = 0.1
 ROWS, COLS = 8, 128
 
-E, W, N, S, NE, NW, SE, SW = range(8)
-WAY = ((0, 1), (0, -1), (1, 0), (-1, 0), (1, 1), (1, -1), (-1, 1), (-1, -1))
-OPPOSITE = (W, E, S, N, SW, SE, NW, NE)
+W, S, E, N, NE, NW, SE, SW = range(8)
+WAY = ((0, -1), (-1, 0), (0, 1), (1, 0), (1, 1), (1, -1), (-1, 1), (-1, -1))
+OPPOSITE = (E, N, W, S, SW, SE, NW, NE)
+
 
 def turn(x, shift, axis):
     return pltpu.roll(x, shift % x.shape[axis], axis)
@@ -42,19 +43,30 @@
     )
 
 
-def spread_out(px, pb, pv, qv, qc, qu):
-    c1 = qc + north(qc)
-    b1 = pb + south(pb)
-    gu = 0.5 * (east(px) - west(px) + north(pv) - south(pv)) + 0.25 * (c1 + west(c1))
-    gv = 0.5 * (north(qv) - south(qv) + east(qu) - west(qu)) + 0.25 * (b1 + east(b1))
-    return gu[:ROWS, :COLS], gv[:ROWS, :COLS]
+CROSS = ((0, 0), (0, 1), (0, -1), (1, 0), (-1, 0))
+U_CORNERS = ((0, 0), (0, -1), (1, 0), (1, -1))
+V_CORNERS = ((0, 0), (0, 1), (-1, 0), (-1, 1))
+
+
+def seen(x, place):
+    dy, dx = place
+    x = turn(x, -dx, 1) if dx else x
+    x = turn(x, -dy, 0) if dy else x
+    return x[:ROWS, :COLS]
+
+
+def gather(weights, values):
+    total = weights[0] * values[0]
+    for a, b in zip(weights[1:], values[1:]):
+        total = total + a * b
+    return total
 
 
 def kernel(
     levels, n_ty, n_tx,
     u_hbm, v_hbm, t_hbm, count_hbm, us_hbm, vs_hbm, ts_hbm, elev_hbm,
     gu_ref, gv_ref, gt_ref, eta_ref, slope_ref,
-    k_pu, k_pv, k_b, k_qv, k_qu, k_c, k_u, k_v,
+    u_weights, v_weights,
     u_ref, v_ref, t_ref, us_ref, vs_ref, ts_ref, count_ref, elev_ref,
     count_in, elev_in, col_out, col_in,
     colp_out, colp_in, corner_in, rown_out, rows_out, rown2_out, rows2_out, row_in, row2_in,
@@ -129,8 +141,11 @@
 
     pl.semaphore_wait(barrier, (n_tx - 1) + (n_ty - 1) + 4)
 
-    for d in range(8):
+    for d in (N, E):
         hop(0, count_ref, count_in.at[OPPOSITE[d]], d).start()
+    for d in (NE, NW, SE, SW, S, W):
+        hop(11, count_ref, count_in.at[OPPOSITE[d]], d).start()
+    for d in (NE, NW, SE, SW, S, W, N, E):
         hop(1, elev_ref, elev_in.at[OPPOSITE[d]], d).start()
 
     wide_row = lax.broadcasted_iota(jnp.int32, (3 * ROWS, 2 * COLS), 0)
@@ -145,15 +160,12 @@
             [jnp.concatenate([a, b], axis=1) for a, b in zip((own, part(N), part(S)), rim)], axis=0
         )
 
-    whole(0, count_in).wait_recv()
-    whole(1, elev_in).wait_recv()
-    count = jnp.where(inside, around(count_ref[...], lambda d: count_in[d]).astype(jnp.float32), 0.0)
-    count_u = jnp.minimum(count, west(count))
-    count_v = jnp.minimum(count, south(count))
-    depth_u = count_u + count_u * (count_u - 1.0) * (0.5 / levels)
-    depth_v = count_v + count_v * (count_v - 1.0) * (0.5 / levels)
-
-    own_u, own_v = count_u[:ROWS, :COLS], count_v[:ROWS, :COLS]
+    whole(0, count_in.at[0:2]).wait_recv()
+    own_count = count_ref[...]
+    own_u = jnp.minimum(own_count, jnp.where(lane == 0, west(count_in[W]), west(own_count))).astype(jnp.float32)
+    own_v = jnp.minimum(own_count, jnp.where(sub == 0, south(count_in[S]), south(own_count))).astype(jnp.float32)
+    own_u = jnp.where((lane == 0) & (c == 0), 0.0, own_u)
+    own_v = jnp.where((sub == 0) & (r == 0), 0.0, own_v)
     col_u = jnp.zeros((ROWS, COLS), jnp.float32)
     col_v = jnp.zeros((ROWS, COLS), jnp.float32)
     for k in range(levels):
@@ -161,7 +173,7 @@
         col_v = col_v + jnp.where(own_v > float(k), vs_ref[k], 0.0)
     col_out[0] = col_u
     col_out[1] = col_v
-    for d in range(8):
+    for d in (NE, NW, SE, SW, N, S, E, W):
         hop(2, col_out, col_in.at[OPPOSITE[d]], d).start()
 
     hop(3, rown_out, row_in.at[1], N).start()
@@ -169,7 +181,7 @@
     hop(4, rown2_out, row2_in.at[1], N).start()
     hop(4, rows2_out, row2_in.at[0], S).start()
     for d in (E, W):
-        hop(5, colp_out, colp_in.at[OPPOSITE[d]], d).start()
+        hop(5, colp_out, colp_in.at[0 if d == E else 1], d).start()
     for d in (NE, NW, SE, SW):
         hop(6, colp_out.at[0:4], corner_in.at[OPPOSITE[d] - NE], d).start()
 
@@ -177,6 +189,13 @@
         low = lax.broadcasted_iota(jnp.int32, (ROWS, 2 * COLS), 0) < 4
         return jnp.concatenate([x[:ROWS], jnp.where(low, x[ROWS : 2 * ROWS], x[2 * ROWS :])], axis=0)
 
+    whole(11, count_in.at[2:8]).wait_recv()
+    whole(1, elev_in).wait_recv()
+    count = jnp.where(inside, around(count_ref[...], lambda d: count_in[d]).astype(jnp.float32), 0.0)
+    count_u = jnp.minimum(count, west(count))
+    count_v = jnp.minimum(count, south(count))
+    depth_u = count_u + count_u * (count_u - 1.0) * (0.5 / levels)
+    depth_v = count_v + count_v * (count_v - 1.0) * (0.5 / levels)
     cu, cv = squeeze(count_u), squeeze(count_v)
     row16 = lax.broadcasted_iota(jnp.int32, (2 * ROWS, 2 * COLS), 0)
     row16 = (r * ROWS + jnp.where(row16 < 12, row16, row16 - 16)).astype(jnp.float32)
@@ -248,7 +267,7 @@
         for number, ref in ((3, row_in), (4, row2_in), (5, colp_in), (6, corner_in)):
             whole(number, ref).wait_recv()
         for f in range(6):
-            side = jnp.where(inner, colp_in[W, f], colp_in[E, f])
+            side = jnp.where(inner, colp_in[0, f], colp_in[1, f])
             sides[f] = jnp.where(beside, side, 0.0)
         for f in range(4):
             upper = jnp.where(inner, corner_in[NW - NE, f], corner_in[NE - NE, f])
@@ -300,23 +319,30 @@
         pair_v, pair_u = v + vn, u + ue
         v_bar = 0.25 * (pair_v + west(pair_v))
         u_bar = 0.25 * (pair_u + south(pair_u))
-        kpu = mask_u * u
-        kpv = mask_u * v_bar
-        kb = mask_u * (fu - 0.5 * (north(u) - south(u)))
-        kqv = mask_v * v
-        kqu = mask_v * u_bar
-        kc = -mask_v * (fv + 0.5 * (east(v) - west(v)))
-        k_pu[k], k_pv[k], k_b[k] = kpu, kpv, kb
-        k_qv[k], k_qu[k], k_c[k] = kqv, kqu, kc
+        ahead_x = 0.5 * mask_u * u
+        ahead_y = 0.5 * mask_u * v_bar
+        turning = 0.25 * mask_u * (fu - 0.5 * (north(u) - south(u)))
         own_mu, own_mv = mask_u[:ROWS, :COLS], mask_v[:ROWS, :COLS]
         ku = -0.5 * own_mu * (ue - west(u))[:ROWS, :COLS]
         kv = -0.5 * own_mv * (vn - south(v))[:ROWS, :COLS]
-        k_u[k] = ku + jnp.where(own_mu > 0.0, 1.0, 0.0)
-        k_v[k] = kv + jnp.where(own_mv > 0.0, 1.0, 0.0)
-        gu, gv = spread_out(kpu * us, kb * us, kpv * us, kqv * vs, kc * vs, kqu * vs)
-        own_us, own_vs = us_ref[k], vs_ref[k]
-        gu_ref[k] = gu + own_us + own_us * ku + (flux_x * face_x)[:ROWS, :COLS]
-        gv_ref[k] = gv + own_vs + own_vs * kv + (flux_y * face_y)[:ROWS, :COLS]
+        u_cross = [ku, seen(ahead_x, CROSS[1]), -seen(ahead_x, CROSS[2]), seen(ahead_y, CROSS[3]), -seen(ahead_y, CROSS[4])]
+        v_corners = [seen(turning, p) for p in V_CORNERS]
+        ahead_y = 0.5 * mask_v * v
+        ahead_x = 0.5 * mask_v * u_bar
+        turning = -0.25 * mask_v * (fv + 0.5 * (east(v) - west(v)))
+        v_cross = [kv, seen(ahead_x, CROSS[1]), -seen(ahead_x, CROSS[2]), seen(ahead_y, CROSS[3]), -seen(ahead_y, CROSS[4])]
+        u_corners = [seen(turning, p) for p in U_CORNERS]
+        us_at, vs_at = [seen(us, p) for p in CROSS], [seen(vs, p) for p in CROSS]
+        gu = gather(u_cross + u_corners, us_at + [seen(vs, p) for p in U_CORNERS])
+        gv = gather(v_cross + v_corners, vs_at + [seen(us, p) for p in V_CORNERS])
+        gu_ref[k] = gu + us_at[0] + (flux_x * face_x)[:ROWS, :COLS]
+        gv_ref[k] = gv + vs_at[0] + (flux_y * face_y)[:ROWS, :COLS]
+        u_cross[0] = ku + jnp.where(own_mu > 0.0, 1.0, 0.0)
+        v_cross[0] = kv + jnp.where(own_mv > 0.0, 1.0, 0.0)
+        for m, weight in enumerate(u_cross + u_corners):
+            u_weights[k, m] = weight
+        for m, weight in enumerate(v_cross + v_corners):
+            v_weights[k, m] = weight
         return carry
 
     third_of = levels // 3
@@ -371,11 +397,15 @@
     d3 = w0 + beta3 * d2 - alpha3 * (w2 + beta2 * w3)
     answer = x2 + alpha3 * d2 + alpha4 * d3
     eta_ref[...] = answer[:ROWS, :COLS]
-    slope_ref[0] = squeeze(answer - west(answer))
-    slope_ref[1] = squeeze(answer - south(answer))
+    slope_x, slope_y = answer - west(answer), answer - south(answer)
+    for m, (slope, place) in enumerate(
+        [(slope_x, p) for p in CROSS] + [(slope_y, p) for p in U_CORNERS]
+        + [(slope_y, p) for p in CROSS] + [(slope_x, p) for p in V_CORNERS]
+    ):
+        slope_ref[m] = seen(slope, place)
 
     for number, ref in (
-        (0, count_in), (1, elev_in), (2, col_in), (3, row_in), (4, row2_in), (5, colp_in), (6, corner_in),
+        (0, count_in.at[0:2]), (11, count_in.at[2:8]), (1, elev_in), (2, col_in), (3, row_in), (4, row2_in), (5, colp_in), (6, corner_in),
         (7, tx_in.at[0]), (8, tx_in.at[1]), (9, ty_in.at[0]), (10, ty_in.at[1]),
     ):
         whole(number, ref).wait_send()
@@ -383,7 +413,7 @@
 
 def finish(
     levels, pieces,
-    gu_ref, gv_ref, gt_ref, eta_ref, slope_ref, k_pu, k_pv, k_b, k_qv, k_qu, k_c, k_u, k_v,
+    gu_ref, gv_ref, gt_ref, eta_ref, slope_ref, u_weights, v_weights,
     gu_hbm, gv_hbm, gt_hbm, eta_hbm,
     gu_out, gv_out, sems,
 ):
@@ -393,14 +423,12 @@
     ]
     for copy in copies:
         copy.start()
-    slope_x, slope_y = slope_ref[0], slope_ref[1]
+    slopes = [slope_ref[m] for m in range(18)]
 
     def level(k, carry):
         thick = 1.0 + k.astype(jnp.float32) * (1.0 / levels)
-        dx, dy = thick * slope_x, thick * slope_y
-        gu, gv = spread_out(k_pu[k] * dx, k_b[k] * dx, k_pv[k] * dx, k_qv[k] * dy, k_c[k] * dy, k_qu[k] * dy)
-        gu_out[k] = gu_ref[k] + gu + k_u[k] * dx[:ROWS, :COLS]
-        gv_out[k] = gv_ref[k] + gv + k_v[k] * dy[:ROWS, :COLS]
+        gu_out[k] = gu_ref[k] + thick * gather([u_weights[k, m] for m in range(9)], slopes[:9])
+        gv_out[k] = gv_ref[k] + thick * gather([v_weights[k, m] for m in range(9)], slopes[9:])
         return carry
 
     size = levels // pieces
@@ -420,17 +448,17 @@
     f32 = jnp.float32
     block = jax.ShapeDtypeStruct(u.shape, f32)
     face = jax.ShapeDtypeStruct(elevation.shape, f32)
-    around = jax.ShapeDtypeStruct((levels, 2 * ROWS, 2 * COLS), f32)
-    slopes = jax.ShapeDtypeStruct((2, 2 * ROWS, 2 * COLS), f32)
+    weights = jax.ShapeDtypeStruct((levels, 9, ROWS, COLS), f32)
+    slopes = jax.ShapeDtypeStruct((18, ROWS, COLS), f32)
     own = pltpu.VMEM((levels, ROWS, COLS), f32)
     two = pltpu.VMEM((levels, 2, COLS), f32)
     tiles = lambda *n, dtype=f32: pltpu.VMEM((*n, ROWS, COLS), dtype)
     vmem, hbm = pl.BlockSpec(memory_space=pltpu.VMEM), pl.BlockSpec(memory_space=pltpu.HBM)
     parts = pl.pallas_call(
         functools.partial(kernel, levels, n_ty, n_tx),
-        out_shape=(block, block, block, face, slopes) + (around,) * 6 + (block, block),
+        out_shape=(block, block, block, face, slopes, weights, weights),
         in_specs=[hbm] * 8,
-        out_specs=[vmem] * 13,
+        out_specs=[vmem] * 7,
         scratch_shapes=[
             own, own, own, own, own, own, tiles(dtype=jnp.int32), tiles(),
             tiles(8, dtype=jnp.int32), tiles(8), tiles(2), tiles(8, 2),
@@ -441,8 +469,8 @@
             pltpu.VMEM((2, n_tx - 1, 1, COLS), f32),
             pltpu.VMEM((2, n_ty - 1, 1, COLS), f32),
             pltpu.SemaphoreType.DMA((8,)),
-            pltpu.SemaphoreType.DMA((11,)),
-            pltpu.SemaphoreType.DMA((11,)),
+            pltpu.SemaphoreType.DMA((12,)),
+            pltpu.SemaphoreType.DMA((12,)),
         ],
         compiler_params=pltpu.CompilerParams(
             collective_id=0, has_side_effects=True, vmem_limit_bytes=32 * 1024 * 1024
@@ -452,7 +480,7 @@
     return pl.pallas_call(
         functools.partial(finish, levels, pieces),
         out_shape=(block, block, block, face),
-        in_specs=[vmem] * 13,
+        in_specs=[vmem] * 7,
         out_specs=[hbm] * 4,
         scratch_shapes=[own, own, pltpu.SemaphoreType.DMA((2 + 2 * pieces,))],
         compiler_params=pltpu.CompilerParams(vmem_limit_bytes=16 * 1024 * 1024),

time: 51.1 us -> 46.8 us (0.916)
  Pallas kernels: 50.3 us -> 46.1 us
    pallas_call x1, Pallas kernels: 3.38 us -> 1.17 us  [on_device(): pl.pallas_call(functools.partial(finish, levels, pieces), out_shape=(bloc...]
    pallas_call x1, Pallas kernels: 46.9 us -> 44.9 us  [on_device(): pl.pallas_call(functools.partial(kernel, levels, n_ty, n_tx), out_shape=(...]
where the time goes in v3:
time: 46.8 us; the launch traced here: 46.7 us
  Pallas kernels  46.1 us (99%)
  between operations  0.64 us (1%)
    pallas_call x1, Pallas kernels, on_device(): pl.pallas_call(functools.partial(kernel, levels, n_ty, n_tx), out_shape=(...  44.9 us
    pallas_call x1, Pallas kernels, on_device(): pl.pallas_call(functools.partial(finish, levels, pieces), out_shape=(bloc...  1.17 us

profile of v3, /device:TPU:1, one launch (start us, length us, event | category | flops | bytes accessed | tf_op | source)
XLA Modules:
  0.0 46.7 jit_solution(12783690193953791466)
XLA Ops:
  0.6 44.9 %shard_map.111 = (f32[30,8,128]{2,1,0:T(8,128)S(1)}, f32[30,8,128]{2,1,0:T(8,128)S(1)}, f32[30,8,128]{2,1,0:T(8,128)S(1)}, f32[8,128]{1,0:T(8,128)S(1)}, f32[18,...) custom-call(f32[30,8,128]{2,1,0:T(8,128)} %u_hbm.1, f32[30,8,128]{2,1,0:T(8,128)} %v_hbm.1, ...), custom_call_target="tpu_custom_call" | custom-call | tf_op jit(solution)/shard_map/pallas_call | solution.py:457
  45.5 1.2 %shard_map.112 = (f32[30,8,128]{2,1,0:T(8,128)}, f32[30,8,128]{2,1,0:T(8,128)}, f32[30,8,128]{2,1,0:T(8,128)}, f32[8,128]{1,0:T(8,128)}) custom-call(f32[30,8,128]{2,1,0:T(8,128)S(1)} %get-tuple-element.11.gu_ref, f32[30,8,128]{2,1,0:T(8,128)S(1)} %get-tuple-element.12.gv_ref, f32[30,8,128]{2,1,0:T(8,128)S(1)} %get-tuple-element.13.gt_ref, ...), custom_call_target="tpu_custom_call" | custom-call | tf_op jit(solution)/shard_map/pallas_call | solution.py:480

commit v4 on v3

--- a/solution.py
+++ b/solution.py
@@ -210,10 +210,13 @@
         inside, elevation + GRAVITY_DT * (east(col_u) - col_u + north(col_v) - col_v), 0.0
     )
 
-    def operate(p):
+    def beyond_one(p):
         flow_u = depth_u * (p - west(p))
         flow_v = depth_v * (p - south(p))
-        return p - GRAVITY_DT * (east(flow_u) - flow_u + north(flow_v) - flow_v)
+        return -GRAVITY_DT * (east(flow_u) - flow_u + north(flow_v) - flow_v)
+
+    def operate(p):
+        return p + beyond_one(p)
 
     sub16 = lax.broadcasted_iota(jnp.int32, (16, COLS), 0)
     lane16 = lax.broadcasted_iota(jnp.int32, (16, COLS), 1)
@@ -352,20 +355,22 @@
         lax.fori_loop(0, third_of, prepare, 0)
 
     p0 = load
-    p1 = operate(p0)
-    p2 = operate(p1)
+    p1 = beyond_one(p0)
+    p2 = beyond_one(p1)
     row = total(
         0, dots([(p0, p0), (p0, p1), (p1, p1), (p1, p2)]), lambda: None, cover_first
     )
     g00, g01, g11, g12 = [pick(row, m) for m in range(4)]
-    alpha1 = g00 / g01
-    norm1 = g00 - 2.0 * alpha1 * g01 + alpha1 * alpha1 * g11
+    alpha1 = g00 / (g00 + g01)
+    rest1 = g01 / (g00 + g01)
+    norm1 = rest1 * rest1 * g00 - 2.0 * rest1 * alpha1 * g01 + alpha1 * alpha1 * g11
     beta1 = norm1 / g00
-    e0, e1 = 1.0 + beta1, -alpha1
-    alpha2 = norm1 / (e0 * e0 * g01 + 2.0 * e0 * e1 * g11 + e1 * e1 * g12)
-    d1 = e0 * p0 + e1 * p1
+    r_b_r = rest1 * rest1 * g01 - 2.0 * rest1 * alpha1 * g11 + alpha1 * alpha1 * g12
+    alpha2 = norm1 / (norm1 + r_b_r - beta1 * norm1 / alpha1)
+    r1 = rest1 * p0 - alpha1 * p1
+    d1 = r1 + beta1 * p0
     x2 = alpha1 * p0 + alpha2 * d1
-    w0 = (p0 - alpha1 * p1) - alpha2 * (e0 * p1 + e1 * p2)
+    w0 = r1 - alpha2 * (d1 + (rest1 + beta1) * p1 - alpha1 * p2)
 
     w1 = d1
     w2, w3 = operate(w0), operate(w1)

time: 46.8 us -> 46.8 us (level)
  no operation moved by 1% of the time
where the time goes in v4:
time: 46.8 us; the launch traced here: 46.7 us
  Pallas kernels  46.1 us (99%)
  between operations  0.64 us (1%)
    pallas_call x1, Pallas kernels, on_device(): pl.pallas_call(functools.partial(kernel, levels, n_ty, n_tx), out_shape=(...  44.9 us
    pallas_call x1, Pallas kernels, on_device(): pl.pallas_call(functools.partial(finish, levels, pieces), out_shape=(bloc...  1.17 us

profile of v4, /device:TPU:1, one launch (start us, length us, event | category | flops | bytes accessed | tf_op | source)
XLA Modules:
  0.0 46.7 jit_solution(14873779072951146451)
XLA Ops:
  0.6 44.9 %shard_map.111 = (f32[30,8,128]{2,1,0:T(8,128)S(1)}, f32[30,8,128]{2,1,0:T(8,128)S(1)}, f32[30,8,128]{2,1,0:T(8,128)S(1)}, f32[8,128]{1,0:T(8,128)S(1)}, f32[18,...) custom-call(f32[30,8,128]{2,1,0:T(8,128)} %u_hbm.1, f32[30,8,128]{2,1,0:T(8,128)} %v_hbm.1, ...), custom_call_target="tpu_custom_call" | custom-call | tf_op jit(solution)/shard_map/pallas_call | solution.py:462
  45.5 1.2 %shard_map.112 = (f32[30,8,128]{2,1,0:T(8,128)}, f32[30,8,128]{2,1,0:T(8,128)}, f32[30,8,128]{2,1,0:T(8,128)}, f32[8,128]{1,0:T(8,128)}) custom-call(f32[30,8,128]{2,1,0:T(8,128)S(1)} %get-tuple-element.11.gu_ref, f32[30,8,128]{2,1,0:T(8,128)S(1)} %get-tuple-element.12.gv_ref, f32[30,8,128]{2,1,0:T(8,128)S(1)} %get-tuple-element.13.gt_ref, ...), custom_call_target="tpu_custom_call" | custom-call | tf_op jit(solution)/shard_map/pallas_call | solution.py:485
